TPU v7x, 32 devices: a whole 2x2x4 slice. The times are simulated.
32 devices in a mesh: col: 8 (over z, x), row: 4 (over y, core).
Axes of the slice: x: 2, y: 2, z: 4, core: 2. Of those that a mesh axis runs over, the one named last changes fastest.
Arguments:
- position: float32 [128, 16384], P(None, ('col', 'row')), may hold values from -6 to 6
- momentum: float32 [128, 16384], P(None, ('col', 'row')), may hold values from -6 to 6
- row_factors: bfloat16 [16384, 16, 128], P(('col', 'row')), may hold values from -1 to 1
- col_factors: bfloat16 [16384, 16, 128], P(('col', 'row')), may hold values from -1 to 1
- tile_ranks: int32 [16, 16], replicated, may hold values from 16 to 128, as said below
- log_mean: float32 [16384], P(('col', 'row')), may hold values from -0.5 to 0.5
- counts: int32 [16384], P(('col', 'row')), may hold values from 0 to 11
- step_size: float32 [128], replicated, may hold values from 0.1 to 0.3
Outputs:
- new_position: float32 [128, 16384], P(None, ('col', 'row'))
- new_momentum: float32 [128, 16384], P(None, ('col', 'row'))
- energy_change: float32 [128], replicated
Inputs may be any that keep to these rules, and one draw needn't show every extreme that they name: `tile_ranks`: every entry is a multiple of 16; in every draw some tile has rank 16 and some tile has rank 128.
All inputs are finite; a program needn't handle non-finite values.
Results may differ from a plain program's by a relative error of at most 0.004.
Values may be sent and summed in bfloat16 or wider, within the bound.
A program may use at most 128 MiB of HBM per device.

v0:
```python
import jax
import jax.numpy as jnp
from jax import lax
from jax.sharding import PartitionSpec as P


def partner_2(value, axis, stride):
    mask = 2**stride
    pairs = [(source, source ^ mask) for source in range(lax.axis_size(axis))]
    return lax.ppermute(value, axis, pairs)


def on_device(
    position, momentum, row_factors, col_factors, tile_ranks, log_mean, counts, step_size
):
    chains = position.shape[0]
    tile_count = tile_ranks.shape[0]
    ranked = row_factors.shape[2]
    device = lax.axis_index(("col", "row"))
    own_tile = device // 2
    own_half = device % 2
    levels = jnp.arange(ranked, dtype=jnp.int32)
    col_ranks = lax.dynamic_slice_in_dim(tile_ranks, own_tile, 1, 1)[:, 0]
    row_ranks = lax.dynamic_slice_in_dim(tile_ranks, own_tile, 1, 0)[0]
    col_live = (levels[None, :] < col_ranks[:, None]).astype(jnp.float32)[:, :, None]
    row_live = (levels[None, :] < row_ranks[:, None]).astype(jnp.float32)[:, :, None]
    rate_base = counts.astype(jnp.float32)[None, :]

    def deliver(partial_value):
        halved = partial_value.reshape(2 * tile_count, ranked // 2, chains)
        arrived = lax.all_to_all(halved, ("col", "row"), split_axis=0, concat_axis=0, tiled=True)
        summed = arrived.reshape(tile_count, 2, ranked // 2, chains).astype(jnp.float32).sum(axis=1)
        summed = summed.astype(jnp.bfloat16)
        partner = partner_2(summed, "row", 0)
        lower_first = jnp.concatenate([summed, partner], axis=1)
        upper_first = jnp.concatenate([partner, summed], axis=1)
        return jnp.where(own_half == 0, lower_first, upper_first)

    def gradient(values):
        rounded = values.astype(jnp.bfloat16)
        partial_value = jnp.einsum(
            "yik,hy->ikh", col_factors, rounded, preferred_element_type=jnp.float32
        )
        partial_value = (partial_value * col_live).astype(jnp.bfloat16)
        coefficient = deliver(partial_value)
        latent_field = jnp.einsum(
            "xjk,jkh->hx", row_factors, coefficient, preferred_element_type=jnp.float32
        )
        exponent = log_mean[None, :] + latent_field
        intensity = jnp.exp(exponent)
        residual = rate_base - intensity
        adjoint = jnp.einsum(
            "xjk,hx->jkh",
            row_factors,
            residual.astype(jnp.bfloat16),
            preferred_element_type=jnp.float32,
        )
        adjoint = (adjoint * row_live).astype(jnp.bfloat16)
        returned = deliver(adjoint)
        pulled = jnp.einsum(
            "yik,ikh->hy", col_factors, returned, preferred_element_type=jnp.float32
        )
        energy = jnp.sum(intensity - rate_base * exponent + 0.5 * values * values, axis=1)
        return (values - pulled, energy)

    full_step = step_size[:, None]

    def leapfrog(section, carry):
        shifted, moment, start_energy, end_energy = carry
        forces, energy = gradient(shifted)
        weight = jnp.where(section == 1, 1.0, 0.5).astype(jnp.float32)
        moment = moment - weight * full_step * forces
        advance = jnp.where(section < 2, full_step * moment, jnp.zeros_like(moment))
        shifted = shifted + advance
        start_energy = jnp.where(section == 0, energy, start_energy)
        end_energy = jnp.where(section == 2, energy, end_energy)
        return (shifted, moment, start_energy, end_energy)

    empty = jnp.zeros((chains,), jnp.float32)
    shifted, moment, start_energy, end_energy = lax.fori_loop(
        0, 3, leapfrog, (position, momentum, empty, empty)
    )
    kinetic = 0.5 * jnp.sum(moment * moment - momentum * momentum, axis=1)
    change = lax.psum(end_energy - start_energy + kinetic, ("col", "row"))
    return (shifted, moment, change)


def solution(mesh):
    in_specs = (
        P(None, ("col", "row")),
        P(None, ("col", "row")),
        P(("col", "row"), None, None),
        P(("col", "row"), None, None),
        P(),
        P(("col", "row")),
        P(("col", "row")),
        P(),
    )
    out_specs = (P(None, ("col", "row")), P(None, ("col", "row")), P())
    return jax.shard_map(
        on_device, mesh=mesh, in_specs=in_specs, out_specs=out_specs, check_vma=False
    )
```

profile of v0, /device:TPU:0, one launch (start us, length us, event | category | flops | bytes accessed | tf_op | source)
XLA Modules:
  0.0 186.0 jit_solution(8267048132765236905)
XLA Ops:
  0.7 0.7 copy-done
  1.5 2.1 %copy.23 = bf16[512,16,128]{2,0,1:T(8,128)(2,1)S(1)} copy(bf16[512,16,128]{2,1,0:T(8,128)(2,1)} %param.13) | data formatting | bytes 4194304
  3.7 4.4 %copy.24 = bf16[512,16,128]{0,2,1:T(8,128)(2,1)} copy(bf16[512,16,128]{2,1,0:T(8,128)(2,1)} %param.12) | data formatting | bytes 4194304
  8.2 138.8 %while.23 = (s32[]{:T(128)}, f32[128,512]{1,0:T(8,128)S(1)}, f32[128,512]{1,0:T(8,128)S(1)}, f32[128]{0:T(128)S(1)}, f32[128]{0:T(128)S(1)}, /*index=5*/f32[128,...) while((s32[]{:T(128)}, f32[128,512]{1,0:T(8,128)S(1)}, ...), condition=%wide.region_4.5_spmd.clone, body=%wide.region_0.4_spmd.clone.sunk | while | flops 1080828416 | bytes 28880336 | solution.py:80
  8.3 0.9 fusion.47
  9.2 22.7 %all_to_all.30 = bf16[32,64,128]{2,1,0:T(8,128)(2,1)S(1)} all-to-all(bf16[32,64,128]{2,1,0:T(8,128)(2,1)S(1)} %bitcast.77), channel_id=1, replica_groups=mesh['col'=8,'row'=4] {'col','row'}, dimensions={0} | all-to-all | bytes 1048576 | tf_op jit(solution)/shard_map/while/body/eval_jaxpr/all_to_all | solution.py:31
  32.1 1.4 collective-permute-done
  33.6 0.5 fusion.48
  34.1 0.7 fusion.49
  34.8 0.3 multiply_convert_fusion.2
  35.1 18.4 %all_to_all.31 = bf16[32,64,128]{2,1,0:T(8,128)(2,1)S(1)} all-to-all(bf16[32,64,128]{2,1,0:T(8,128)(2,1)S(1)} %bitcast.76), channel_id=1, replica_groups=mesh['col'=8,'row'=4] {'col','row'}, dimensions={0} | all-to-all | bytes 1048576 | tf_op jit(solution)/shard_map/while/body/eval_jaxpr/all_to_all | solution.py:31
  53.7 1.6 collective-permute-done.1
  55.4 2.0 %fusion.50 = (f32[128]{0:T(128)S(1)}, f32[128,512]{1,0:T(8,128)S(1)}, f32[128,512]{1,0:T(8,128)S(1)}) fusion(f32[128,512]{1,0:T(8,128)S(1)} %get-tuple-element.580, f32[128,512]{1,0:T(8,128)S(1)} %fusion.48, f32[512]{0:T(512)S(1)} %bitcast.80, f32[128]{0:T(128)S(1)} %bitcast.82, pred[]{:T(512)S(6)} %lt.137, f32[128,512]{1,0:T(8,128)S(1)} %get-tuple-element.581, ...), kind=kOutput, calls=%fused_computation.29.clone.1 | convolution fusion | flops 271581056 | bytes 3935746 | tf_op jit(solution)/shard_map/while/body/eval_jaxpr/yik,ikh->hy/dot_general | solution.py:60
  57.4 0.9 fusion.47
  58.3 18.4 %all_to_all.30 = bf16[32,64,128]{2,1,0:T(8,128)(2,1)S(1)} all-to-all(bf16[32,64,128]{2,1,0:T(8,128)(2,1)S(1)} %bitcast.77), channel_id=1, replica_groups=mesh['col'=8,'row'=4] {'col','row'}, dimensions={0} | all-to-all | bytes 1048576 | tf_op jit(solution)/shard_map/while/body/eval_jaxpr/all_to_all | solution.py:31
  77.0 1.4 collective-permute-done
  78.4 0.5 fusion.48
  78.9 0.7 fusion.49
  79.6 0.3 multiply_convert_fusion.2
  80.0 18.4 %all_to_all.31 = bf16[32,64,128]{2,1,0:T(8,128)(2,1)S(1)} all-to-all(bf16[32,64,128]{2,1,0:T(8,128)(2,1)S(1)} %bitcast.76), channel_id=1, replica_groups=mesh['col'=8,'row'=4] {'col','row'}, dimensions={0} | all-to-all | bytes 1048576 | tf_op jit(solution)/shard_map/while/body/eval_jaxpr/all_to_all | solution.py:31
  98.5 1.6 collective-permute-done.1
  100.2 1.9 %fusion.50 = (f32[128]{0:T(128)S(1)}, f32[128,512]{1,0:T(8,128)S(1)}, f32[128,512]{1,0:T(8,128)S(1)}) fusion(f32[128,512]{1,0:T(8,128)S(1)} %get-tuple-element.580, f32[128,512]{1,0:T(8,128)S(1)} %fusion.48, f32[512]{0:T(512)S(1)} %bitcast.80, f32[128]{0:T(128)S(1)} %bitcast.82, pred[]{:T(512)S(6)} %lt.137, f32[128,512]{1,0:T(8,128)S(1)} %get-tuple-element.581, ...), kind=kOutput, calls=%fused_computation.29.clone.1 | convolution fusion | flops 271581056 | bytes 3935746 | tf_op jit(solution)/shard_map/while/body/eval_jaxpr/yik,ikh->hy/dot_general | solution.py:60
  102.2 0.9 fusion.47
  103.2 18.4 %all_to_all.30 = bf16[32,64,128]{2,1,0:T(8,128)(2,1)S(1)} all-to-all(bf16[32,64,128]{2,1,0:T(8,128)(2,1)S(1)} %bitcast.77), channel_id=1, replica_groups=mesh['col'=8,'row'=4] {'col','row'}, dimensions={0} | all-to-all | bytes 1048576 | tf_op jit(solution)/shard_map/while/body/eval_jaxpr/all_to_all | solution.py:31
  121.8 1.4 collective-permute-done
  123.2 0.5 fusion.48
  123.7 0.7 fusion.49
  124.4 0.3 multiply_convert_fusion.2
  124.8 18.4 %all_to_all.31 = bf16[32,64,128]{2,1,0:T(8,128)(2,1)S(1)} all-to-all(bf16[32,64,128]{2,1,0:T(8,128)(2,1)S(1)} %bitcast.76), channel_id=1, replica_groups=mesh['col'=8,'row'=4] {'col','row'}, dimensions={0} | all-to-all | bytes 1048576 | tf_op jit(solution)/shard_map/while/body/eval_jaxpr/all_to_all | solution.py:31
  143.4 1.6 collective-permute-done.1
  145.0 2.0 %fusion.50 = (f32[128]{0:T(128)S(1)}, f32[128,512]{1,0:T(8,128)S(1)}, f32[128,512]{1,0:T(8,128)S(1)}) fusion(f32[128,512]{1,0:T(8,128)S(1)} %get-tuple-element.580, f32[128,512]{1,0:T(8,128)S(1)} %fusion.48, f32[512]{0:T(512)S(1)} %bitcast.80, f32[128]{0:T(128)S(1)} %bitcast.82, pred[]{:T(512)S(6)} %lt.137, f32[128,512]{1,0:T(8,128)S(1)} %get-tuple-element.581, ...), kind=kOutput, calls=%fused_computation.29.clone.1 | convolution fusion | flops 271581056 | bytes 3935746 | tf_op jit(solution)/shard_map/while/body/eval_jaxpr/yik,ikh->hy/dot_general | solution.py:60
  147.1 38.9 %psum.7 = f32[128]{0:T(128)} all-reduce(f32[128]{0:T(128)S(1)} %multiply_add_fusion), channel_id=1, replica_groups=mesh['col'=8,'row'=4] {'col','row'}, use_global_device_ids=true, to_apply=%region_6.7 | all-reduce | flops 128 | bytes 1024 | tf_op jit(solution)/shard_map/psum | solution.py:84
  (54 shorter events, 1.8 us)
Async XLA Ops:
  0.6 0.7 copy-start
  3.7 4.4 %copy-start.7 = (s32[512]{0:T(512)S(1)}, s32[512]{0:T(512)}, u32[]{:S(2)}) copy-start(s32[512]{0:T(512)} %param.16) | copy-start | bytes 6148
  3.7 4.4 %copy-start.3 = (f32[128,512]{1,0:T(8,128)S(1)}, f32[128,512]{1,0:T(8,128)}, u32[]{:S(2)}) copy-start(f32[128,512]{1,0:T(8,128)} %param.10) | copy-start | bytes 786436
  3.7 4.4 %copy-start.6 = (f32[128,512]{1,0:T(8,128)S(1)}, f32[128,512]{1,0:T(8,128)}, u32[]{:S(2)}) copy-start(f32[128,512]{1,0:T(8,128)} %param.11) | copy-start | bytes 786436
  3.7 4.4 %copy-start.8 = (f32[512]{0:T(512)S(1)}, f32[512]{0:T(512)}, u32[]{:S(2)}) copy-start(f32[512]{0:T(512)} %param.15) | copy-start | bytes 6148
  3.7 4.4 %copy-start.9 = (f32[128]{0:T(128)S(1)}, f32[128]{0:T(128)}, u32[]{:S(2)}) copy-start(f32[128]{0:T(128)} %param.17) | copy-start | bytes 1540
  8.2 138.9 %copy-start.4 = (f32[128,512]{1,0:T(8,128)S(1)}, f32[128,512]{1,0:T(8,128)}, u32[]{:S(2)}) copy-start(f32[128,512]{1,0:T(8,128)} %param.11) | copy-start | bytes 786436
  8.3 25.4 %copy-start.1 = (bf16[512,16,128]{0,2,1:T(8,128)(2,1)S(1)}, bf16[512,16,128]{0,2,1:T(8,128)(2,1)}, u32[]{:S(2)}) copy-start(bf16[512,16,128]{0,2,1:T(8,128)(2,1)} %get-tuple-element.607) | copy-start | bytes 6291460 | tf_op jit(solution)/shard_map/while
  32.0 1.6 collective-permute-start
  53.6 1.7 collective-permute-start.1
  57.4 21.0 %copy-start.1 = (bf16[512,16,128]{0,2,1:T(8,128)(2,1)S(1)}, bf16[512,16,128]{0,2,1:T(8,128)(2,1)}, u32[]{:S(2)}) copy-start(bf16[512,16,128]{0,2,1:T(8,128)(2,1)} %get-tuple-element.607) | copy-start | bytes 6291460 | tf_op jit(solution)/shard_map/while
  76.8 1.6 collective-permute-start
  98.4 1.7 collective-permute-start.1
  102.2 21.0 %copy-start.1 = (bf16[512,16,128]{0,2,1:T(8,128)(2,1)S(1)}, bf16[512,16,128]{0,2,1:T(8,128)(2,1)}, u32[]{:S(2)}) copy-start(bf16[512,16,128]{0,2,1:T(8,128)(2,1)} %get-tuple-element.607) | copy-start | bytes 6291460 | tf_op jit(solution)/shard_map/while
  121.6 1.6 collective-permute-start
  143.3 1.7 collective-permute-start.1
  147.0 39.1 %copy-start.2 = (f32[128,512]{1,0:T(8,128)}, f32[128,512]{1,0:T(8,128)S(1)}, u32[]{:S(2)}) copy-start(f32[128,512]{1,0:T(8,128)S(1)} %get-tuple-element.347) | copy-start | bytes 786436
  147.0 39.0 %copy-start.5 = (f32[128,512]{1,0:T(8,128)}, f32[128,512]{1,0:T(8,128)S(1)}, u32[]{:S(2)}) copy-start(f32[128,512]{1,0:T(8,128)S(1)} %get-tuple-element.348) | copy-start | bytes 786436
where the time goes:
time: 187 us; the launch traced here: 186 us
  blocking collectives  154 us (82%)
  matrix products  12.1 us (6%)
  waiting for transfers between devices  9.24 us (5%)
  local copies, waits for them, and re-layouts  7.44 us (4%)
  other arithmetic  2.09 us (1%)
    all_to_all x6, blocking collectives, deliver(): lax.all_to_all(halved, ('col', 'row'), split_axis=0, concat_axis=0, tiled...  115 us
    psum x1, blocking collectives, on_device(): change = lax.psum(end_energy - start_energy + kinetic, ('col', 'row'))  38.9 us
    ppermute x6, waiting for transfers between devices, partner_2(): return lax.ppermute(value, axis, pairs)  9.24 us
    unnamed x20, local copies, waits for them, and re-layouts  7.24 us
    dot_general x3, matrix products, gradient(): jnp.einsum('yik,ikh->hy', col_factors, returned, preferred_element_type=j...  5.85 us
  transfers between devices with their start and end apart: 6, of which 6 were waited for; matrix products, arithmetic and copies ran while one was open for 0% of the time, Pallas kernels for 0%

commit v1 on v0

v1 whole, which is shorter than its diff:
```python
import functools

import jax
import jax.numpy as jnp
from jax import lax
from jax.experimental import pallas as pl
from jax.experimental.pallas import tpu as pltpu
from jax.sharding import PartitionSpec as P

MESH = pl.DeviceIdType.MESH
GROUPS = 2
SWAP = jnp.bfloat16
FULL = jnp.float32
HALF = jnp.bfloat16
FORWARD, BACKWARD = 0, 1


def kernel(
    row_size,
    pos, mom, col2, row2, log_mean, counts, step,
    new_pos, new_mom, energy,
    zs, ps, col_far, row_far, lm_far, cnt_far,
    out_buf, in_buf, swap_out, swap_in, gain,
    e_own, e_far, e_chip, e_all, e_part, e_rest,
    init_send, init_recv, send, recv, swap_send, swap_recv,
    tail_send, tail_recv, all_send, all_recv,
):
    halves = in_buf.shape[2]
    chains, cells = pos.shape
    ranked = in_buf.shape[4]
    block = chains // GROUPS

    me = lax.axis_index("col") * row_size + lax.axis_index("row")
    tile = me // 2
    core = me % 2
    side = tile % 2
    slot = tile // 2

    def address(index):
        return (index // row_size, index % row_size)

    partner = address(2 * tile + 1 - core)

    def peer(m):
        return address(2 * (2 * m + core) + side)

    def each_peer(action, at_home=None):
        def body(n, carry):
            action((slot + 1 + n) % halves)
            return carry

        lax.fori_loop(0, halves - 1, body, 0)

        @pl.when(core != side)
        def _():
            action(slot)

        if at_home is not None:
            @pl.when(core == side)
            def _():
                at_home()

    barrier = pltpu.get_barrier_semaphore()

    def greet(m):
        pl.semaphore_signal(barrier, inc=1, device_id=peer(m), device_id_type=MESH)

    each_peer(greet)
    pl.semaphore_signal(barrier, inc=1, device_id=partner, device_id_type=MESH)
    pl.semaphore_wait(barrier, halves + jnp.where(core == side, 0, 1))

    def remote(src, dst, s, r, where):
        return pltpu.make_async_remote_copy(
            src_ref=src, dst_ref=dst, send_sem=s, recv_sem=r,
            device_id=where, device_id_type=MESH,
        )

    first = [
        remote(src, dst, init_send.at[n], init_recv.at[n], partner)
        for n, (src, dst) in enumerate([
            (pos, zs.at[1]), (col2.at[1 - core], col_far),
            (log_mean, lm_far), (counts, cnt_far),
            (row2.at[1 - core], row_far), (mom, ps.at[1]),
        ])
    ]
    for copy in first:
        copy.start()
    zs[0] = pos[...]
    ps[0] = mom[...]
    gain[...] = jnp.zeros_like(gain)

    def rows(g):
        return pl.ds(g * block, block)

    def project(way, g, near, far, near_ref, far_ref):
        result = jnp.dot(near, near_ref[core], preferred_element_type=FULL)
        result += jnp.dot(far, far_ref[...], preferred_element_type=FULL)
        result = result.astype(HALF)
        for m in range(halves):
            out_buf[way, g, m] = result[:, m * ranked:(m + 1) * ranked]

        def start(m):
            remote(
                out_buf.at[way, g, m], in_buf.at[way, g, slot],
                send.at[way, g, m], recv.at[way, g, slot], peer(m),
            ).start()

        def keep():
            in_buf[way, g, slot] = out_buf[way, g, slot]

        each_peer(start, keep)

    def expand(way, g, near_ref, far_ref):
        def finish(m):
            copy = remote(
                out_buf.at[way, g, m], in_buf.at[way, g, m],
                send.at[way, g, m], recv.at[way, g, m], peer(m),
            )
            copy.wait_recv()
            copy.wait_send()

        each_peer(finish)
        held = jnp.concatenate([in_buf[way, g, m] for m in range(halves)], axis=1)
        dims = (((1,), (1,)), ((), ()))
        copies = []
        far = lax.dot_general(held, far_ref[...], dims, preferred_element_type=FULL)
        swap_out[way, g, 1] = far.astype(SWAP)
        copies.append(remote(
            swap_out.at[way, g, 1], swap_in.at[way, g, 0],
            swap_send.at[way, g, 0], swap_recv.at[way, g, 0], partner,
        ))
        copies[0].start()
        near = lax.dot_general(held, near_ref[core], dims, preferred_element_type=FULL)
        swap_out[way, g, 0] = near.astype(SWAP)
        copies.append(remote(
            swap_out.at[way, g, 0], swap_in.at[way, g, 1],
            swap_send.at[way, g, 1], swap_recv.at[way, g, 1], partner,
        ))
        copies[1].start()
        for copy in copies:
            copy.wait()
        near = near + swap_in[way, g, 0].astype(FULL)
        far = far + swap_in[way, g, 1].astype(FULL)
        return near, far

    def send_forward(g):
        project(
            FORWARD, g,
            zs[0, rows(g)].astype(HALF), zs[1, rows(g)].astype(HALF),
            col2, col_far,
        )

    first[0].wait()
    first[1].wait()
    for g in range(GROUPS):
        send_forward(g)
    for copy in first[2:]:
        copy.wait()

    def section(at, carry):
        sign = (at // 2 - (2 - at) // 2).astype(FULL)
        weight = jnp.where(at == 1, 1.0, 0.5).astype(FULL)
        for g in range(GROUPS):
            near, far = expand(FORWARD, g, row2, row_far)
            exponent = log_mean[...] + near
            intensity = jnp.exp(exponent)
            rate = counts[...].astype(FULL)
            residual = (rate - intensity).astype(HALF)
            residual_far = (
                cnt_far[...].astype(FULL) - jnp.exp(lm_far[...] + far)
            ).astype(HALF)
            project(BACKWARD, g, residual, residual_far, row2, row_far)
            values = zs[0, rows(g)]
            gain[rows(g)] += sign * (
                intensity - rate * exponent + 0.5 * values * values
            )
        for g in range(GROUPS):
            pulled = expand(BACKWARD, g, col2, col_far)
            size = step[rows(g)]
            for part in range(2):
                values = zs[part, rows(g)]
                moment = ps[part, rows(g)] - weight * size * (values - pulled[part])
                ps[part, rows(g)] = moment

                @pl.when(at < 2)
                def _():
                    zs[part, rows(g)] = values + size * moment

            @pl.when(at < 2)
            def _():
                send_forward(g)

        return carry

    lax.fori_loop(0, 3, section, 0)

    after = ps[0]
    before = mom[...]
    change = gain[...] + 0.5 * (after * after - before * before)
    lanes = e_own.shape[1]
    change = sum(change[:, n * lanes:(n + 1) * lanes] for n in range(cells // lanes))
    total = jnp.sum(change.T, axis=0, keepdims=True)
    e_own[...] = jnp.broadcast_to(total, e_own.shape)
    copy = remote(e_own, e_far, tail_send.at[0], tail_recv.at[0], partner)
    copy.start()
    new_pos[...] = zs[0]
    new_mom[...] = after
    copy.wait()
    e_chip[...] = e_own[...] + e_far[...]

    def spread(m):
        remote(
            e_chip, e_all.at[slot], all_send.at[m], all_recv.at[slot], peer(m)
        ).start()

    def spread_home():
        e_all[slot] = e_chip[...]

    def gather(m):
        copy = remote(e_chip, e_all.at[m], all_send.at[m], all_recv.at[m], peer(m))
        copy.wait_recv()
        copy.wait_send()

    each_peer(spread, spread_home)
    each_peer(gather)
    e_part[...] = jnp.sum(e_all[...], axis=0)
    copy = remote(e_part, e_rest, tail_send.at[1], tail_recv.at[1], partner)
    copy.start()
    copy.wait()
    energy[...] = e_part[...] + e_rest[...]


def on_device(
    row_size,
    position, momentum, row_factors, col_factors, tile_ranks, log_mean, counts, step_size
):
    chains, cells = position.shape
    tiles = tile_ranks.shape[0]
    halves = tiles // 2
    ranked = row_factors.shape[2]
    device = lax.axis_index(("col", "row"))
    tile = device // 2
    levels = jnp.arange(ranked, dtype=jnp.int32)
    col_ranks = lax.dynamic_slice_in_dim(tile_ranks, tile, 1, 1)[:, 0]
    row_ranks = lax.dynamic_slice_in_dim(tile_ranks, tile, 1, 0)[0]

    def prepare(factors, ranks):
        live = levels[None, :] < ranks[:, None]
        kept = jnp.where(live[None], factors, jnp.zeros_like(factors))
        kept = kept.reshape(cells, halves, 2, ranked)
        return jnp.transpose(kept, (2, 0, 1, 3)).reshape(2, cells, halves * ranked)

    block = chains // GROUPS
    vmem = pl.BlockSpec(memory_space=pltpu.VMEM)
    dma = pltpu.SemaphoreType.DMA
    small = pltpu.VMEM((8, chains), FULL)
    new_pos, new_mom, energy = pl.pallas_call(
        functools.partial(kernel, row_size),
        out_shape=(
            jax.ShapeDtypeStruct(position.shape, FULL),
            jax.ShapeDtypeStruct(position.shape, FULL),
            jax.ShapeDtypeStruct((8, chains), FULL),
        ),
        in_specs=[vmem] * 7,
        out_specs=(vmem, vmem, vmem),
        scratch_shapes=[
            pltpu.VMEM((2, chains, cells), FULL),
            pltpu.VMEM((2, chains, cells), FULL),
            pltpu.VMEM((cells, halves * ranked), HALF),
            pltpu.VMEM((cells, halves * ranked), HALF),
            pltpu.VMEM((1, cells), FULL),
            pltpu.VMEM((1, cells), jnp.int32),
            pltpu.VMEM((2, GROUPS, halves, block, ranked), HALF),
            pltpu.VMEM((2, GROUPS, halves, block, ranked), HALF),
            pltpu.VMEM((2, GROUPS, 2, block, cells), SWAP),
            pltpu.VMEM((2, GROUPS, 2, block, cells), SWAP),
            pltpu.VMEM((chains, cells), FULL),
            small, small, small,
            pltpu.VMEM((halves, 8, chains), FULL),
            small, small,
            dma((6,)), dma((6,)),
            dma((2, GROUPS, halves)), dma((2, GROUPS, halves)),
            dma((2, GROUPS, 2)), dma((2, GROUPS, 2)),
            dma((2,)), dma((2,)),
            dma((halves,)), dma((halves,)),
        ],
        compiler_params=pltpu.CompilerParams(collective_id=0, has_side_effects=True),
    )(
        position, momentum,
        prepare(col_factors, col_ranks), prepare(row_factors, row_ranks),
        log_mean[None, :], counts[None, :], step_size[:, None],
    )
    return new_pos, new_mom, energy[0]


def solution(mesh):
    in_specs = (
        P(None, ("col", "row")),
        P(None, ("col", "row")),
        P(("col", "row"), None, None),
        P(("col", "row"), None, None),
        P(),
        P(("col", "row")),
        P(("col", "row")),
        P(),
    )
    out_specs = (P(None, ("col", "row")), P(None, ("col", "row")), P())
    return jax.shard_map(
        functools.partial(on_device, mesh.shape["row"]),
        mesh=mesh, in_specs=in_specs, out_specs=out_specs, check_vma=False,
    )
```

time: 187 us -> 87.4 us (0.47)
  blocking collectives: 154 us -> 0 us
  Pallas kernels: 0 us -> 71.5 us
  matrix products: 12.1 us -> 0 us
  waiting for transfers between devices: 9.24 us -> 0 us
  local copies, waits for them, and re-layouts: 7.44 us -> 11.3 us
    all_to_all x6 -> x0, blocking collectives: 115 us -> none  [deliver(): lax.all_to_all(halved, ('col', 'row'), split_axis=0, concat_axis=0, tiled...]
    pallas_call x0 -> x1, Pallas kernels: none -> 71.5 us  [on_device(): pl.pallas_call(functools.partial(kernel, row_size), out_shape=(jax.ShapeD...]
    psum x1 -> x0, blocking collectives: 38.9 us -> none  [on_device(): change = lax.psum(end_energy - start_energy + kinetic, ('col', 'row'))]
    dot_general x9 -> x0, matrix products: 9.99 us -> none  [the longest x3 5.85 us: gradient(): jnp.einsum('yik,ikh->hy', col_factors, returned, preferred_element_type=j...]
    ppermute x6 -> x0, waiting for transfers between devices: 9.24 us -> none  [partner_2(): return lax.ppermute(value, axis, pairs)]
    reshape x0 -> x4, local copies, waits for them, and re-layouts: none -> 5.19 us  [the longest x2 4.65 us: prepare(): return jnp.transpose(kept, (2, 0, 1, 3)).reshape(2, cells, halves * ranked)]
    select_n x3 -> x2, other arithmetic: 0.04 us -> 3.46 us  [prepare(): kept = jnp.where(live[None], factors, jnp.zeros_like(factors))]
    unnamed x20 -> x6, local copies, waits for them, and re-layouts: 7.24 us -> 4.02 us
  transfers between devices with their start and end apart: 6 -> 0, of which waited for: 6 -> 0; matrix products, arithmetic and copies ran while one was open for 0% -> 0% of each run, Pallas kernels for 0% -> 0%
where the time goes in v1:
time: 87.4 us; the launch traced here: 87.1 us
  Pallas kernels  71.5 us (82%)
  local copies, waits for them, and re-layouts  11.3 us (13%)
  other arithmetic  3.62 us (4%)
    pallas_call x1, Pallas kernels, on_device(): pl.pallas_call(functools.partial(kernel, row_size), out_shape=(jax.ShapeD...  71.5 us
    reshape x2, local copies, waits for them, and re-layouts, prepare(): return jnp.transpose(kept, (2, 0, 1, 3)).reshape(2, cells, halves * ranked)  4.65 us
    unnamed x6, local copies, waits for them, and re-layouts  4.02 us
    select_n x2, other arithmetic, prepare(): kept = jnp.where(live[None], factors, jnp.zeros_like(factors))  3.46 us

profile of v1, /device:TPU:0, one launch (start us, length us, event | category | flops | bytes accessed | tf_op | source)
XLA Modules:
  0.0 87.1 jit_solution(1493277735220287268)
XLA Ops:
  0.6 0.0 copy-start
  0.7 0.7 copy-done
  1.3 0.2 dynamic-slice_reduce_fusion
  1.5 0.1 iota_compare_fusion.1
  1.6 1.7 %broadcast_select_fusion.1 = bf16[512,16,128]{2,1,0:T(8,128)(2,1)S(1)} fusion(bf16[512,16,128]{2,1,0:T(8,128)(2,1)} %param.11, pred[16,128]{1,0:T(8,128)(4,1)S(1)} %iota_compare_fusion.1), kind=kLoop, calls=%fused_computation.3 | loop fusion | flops 1048576 | bytes 4196352 | tf_op jit(solution)/shard_map/jit(_where)/select_n | solution.py:249
  3.3 0.3 copy.20
  3.6 2.3 %reshape.59.col2 = bf16[2,512,1024]{2,1,0:T(8,128)(2,1)} reshape(bf16[2,512,8,128]{3,2,1,0:T(8,128)(2,1)S(1)} %bitcast.20) | data formatting | bytes 4194304 | tf_op jit(solution)/shard_map/reshape | solution.py:251
  5.9 0.1 iota_compare_fusion
  6.0 1.7 %broadcast_select_fusion = bf16[512,16,128]{2,1,0:T(8,128)(2,1)S(1)} fusion(bf16[512,16,128]{2,1,0:T(8,128)(2,1)} %param.10, pred[16,128]{1,0:T(8,128)(4,1)S(1)} %iota_compare_fusion), kind=kLoop, calls=%fused_computation.2 | loop fusion | flops 1048576 | bytes 4196352 | tf_op jit(solution)/shard_map/jit(_where)/select_n | solution.py:249
  7.7 0.3 copy.19
  8.0 0.0 copy-start.1
  8.0 2.3 %reshape.61.row2 = bf16[2,512,1024]{2,1,0:T(8,128)(2,1)} reshape(bf16[2,512,8,128]{3,2,1,0:T(8,128)(2,1)S(1)} %bitcast.22) | data formatting | bytes 4194304 | tf_op jit(solution)/shard_map/reshape | solution.py:251
  10.4 0.0 copy-done.1
  10.4 0.7 copy.16.step
  11.1 71.5 %shard_map.103 = (f32[128,512]{1,0:T(8,128)}, f32[128,512]{1,0:T(8,128)}, f32[8,128]{1,0:T(8,128)}) custom-call(f32[128,512]{1,0:T(8,128)} %pos.1, f32[128,512]{1,0:T(8,128)} %mom.1, bf16[2,512,1024]{2,1,0:T(8,128)(2,1)} %reshape.59.col2, bf16[2,512,1024]{2,1,0:T(8,128)(2,1)} %reshape.61.row2, f32[1,512]{1,0:T(1,128)} %bitcast.23, s32[1,512]{1,0:T(1,128)} %bitcast.24, ...), custom_call_target="tpu_custom_call" | custom-call | tf_op jit(solution)/shard_map/pallas_call | solution.py:257
  82.6 1.2 %slice_bitcast_fusion = f32[128]{0:T(128)} fusion(f32[8,128]{1,0:T(8,128)} %get-tuple-element.8), kind=kLoop, calls=%fused_computation.7 | loop fusion | bytes 1024 | tf_op jit(solution)/shard_map/squeeze | solution.py:293
  83.8 1.7 %copy.23 = f32[128,512]{1,0:T(8,128)} copy(f32[128,512]{1,0:T(8,128)} %get-tuple-element.12) | data formatting | bytes 524288
  85.5 1.7 %copy.24 = f32[128,512]{1,0:T(8,128)} copy(f32[128,512]{1,0:T(8,128)} %get-tuple-element.13) | data formatting | bytes 524288
  (1 shorter events, 0.0 us)
Async XLA Ops:
  0.6 0.7 copy-start
  8.0 2.3 %copy-start.1 = (f32[128]{0:T(128)S(1)}, f32[128]{0:T(128)}, u32[]{:S(2)}) copy-start(f32[128]{0:T(128)} %param.15) | copy-start | bytes 1540

commit v2 on v1

--- a/solution.py
+++ b/solution.py
@@ -17,12 +17,13 @@
 
 def kernel(
     row_size,
-    pos, mom, col2, row2, log_mean, counts, step,
-    new_pos, new_mom, energy,
-    zs, ps, col_far, row_far, lm_far, cnt_far,
+    pos, mom, col_raw, row_raw, ranks, log_mean, counts, step_row,
+    last_pos, mid_mom, last_force, energy, energy_rest,
+    zs, ps, raw, col2, row2, col_far, row_far, lm_far, cnt_far, live, step,
+    pre_out, pre_in,
     out_buf, in_buf, swap_out, swap_in, gain,
     e_own, e_far, e_chip, e_all, e_part, e_rest,
-    init_send, init_recv, send, recv, swap_send, swap_recv,
+    raw_sem, init_send, init_recv, pre_send, pre_recv, send, recv, swap_send, swap_recv,
     tail_send, tail_recv, all_send, all_recv,
 ):
     halves = in_buf.shape[2]
@@ -44,12 +45,27 @@
     def peer(m):
         return address(2 * (2 * m + core) + side)
 
+    def flipped(mask):
+        total, bit = 0, 1
+        while bit < halves:
+            low = (slot // bit) % 2
+            total = total + bit * ((1 - low) if mask & bit else low)
+            bit *= 2
+        return total
+
+    unrolled = halves <= 8 and halves & (halves - 1) == 0
+    others = [flipped(mask) for mask in range(halves - 1, 0, -1)] if unrolled else []
+
     def each_peer(action, at_home=None):
-        def body(n, carry):
-            action((slot + 1 + n) % halves)
-            return carry
-
-        lax.fori_loop(0, halves - 1, body, 0)
+        if unrolled:
+            for m in others:
+                action(m)
+        else:
+            def body(n, carry):
+                action((slot + 1 + n) % halves)
+                return carry
+
+            lax.fori_loop(0, halves - 1, body, 0)
 
         @pl.when(core != side)
         def _():
@@ -60,6 +76,8 @@
             def _():
                 at_home()
 
+    fetch = pltpu.make_async_copy(col_raw, raw, raw_sem.at[0])
+    fetch.start()
     barrier = pltpu.get_barrier_semaphore()
 
     def greet(m):
@@ -67,6 +85,40 @@
 
     each_peer(greet)
     pl.semaphore_signal(barrier, inc=1, device_id=partner, device_id_type=MESH)
+    zs[0] = pos[...]
+    ps[0] = mom[...]
+    gain[...] = jnp.zeros_like(gain)
+    step[...] = jnp.broadcast_to(step_row[...], step.shape).T
+    level = lax.broadcasted_iota(jnp.int32, (1, ranked), 1)
+    for m in range(halves):
+        columns = pl.ds(m * ranked, ranked)
+        other = 2 * m + core
+        live[FORWARD, :, columns] = (level < ranks[other, tile]).astype(FULL)
+        live[BACKWARD, :, columns] = (level < ranks[tile, other]).astype(FULL)
+
+    def rows(g):
+        return pl.ds(g * block, block)
+
+    def regroup(target):
+        tiles = raw.shape[1]
+        count = max(16, 1024 // tiles)
+
+        def body(n, carry):
+            some = pl.ds(pl.multiple_of(n * count, count), count)
+            flat = raw[some].reshape(count, tiles * ranked)
+            for parity in range(2):
+                target[parity, some] = jnp.concatenate(
+                    [flat[:, j * ranked:(j + 1) * ranked] for j in range(parity, tiles, 2)],
+                    axis=1,
+                )
+            return carry
+
+        lax.fori_loop(0, cells // count, body, 0)
+
+    fetch.wait()
+    regroup(col2)
+    fetch = pltpu.make_async_copy(row_raw, raw, raw_sem.at[0])
+    fetch.start()
     pl.semaphore_wait(barrier, halves + jnp.where(core == side, 0, 1))
 
     def remote(src, dst, s, r, where):
@@ -75,27 +127,18 @@
             device_id=where, device_id_type=MESH,
         )
 
-    first = [
-        remote(src, dst, init_send.at[n], init_recv.at[n], partner)
-        for n, (src, dst) in enumerate([
-            (pos, zs.at[1]), (col2.at[1 - core], col_far),
-            (log_mean, lm_far), (counts, cnt_far),
-            (row2.at[1 - core], row_far), (mom, ps.at[1]),
-        ])
-    ]
-    for copy in first:
+    def pass_on(n, src, dst):
+        copy = remote(src, dst, init_send.at[n], init_recv.at[n], partner)
         copy.start()
-    zs[0] = pos[...]
-    ps[0] = mom[...]
-    gain[...] = jnp.zeros_like(gain)
-
-    def rows(g):
-        return pl.ds(g * block, block)
+        return copy
 
     def project(way, g, near, far, near_ref, far_ref):
         result = jnp.dot(near, near_ref[core], preferred_element_type=FULL)
         result += jnp.dot(far, far_ref[...], preferred_element_type=FULL)
-        result = result.astype(HALF)
+        dispatch(way, g, result)
+
+    def dispatch(way, g, result):
+        result = (result * live[way]).astype(HALF)
         for m in range(halves):
             out_buf[way, g, m] = result[:, m * ranked:(m + 1) * ranked]
 
@@ -150,11 +193,28 @@
             col2, col_far,
         )
 
-    first[0].wait()
-    first[1].wait()
+    early = []
     for g in range(GROUPS):
-        send_forward(g)
-    for copy in first[2:]:
+        near = zs[0, rows(g)].astype(HALF)
+        pre_out[g] = jnp.dot(near, col2[1 - core], preferred_element_type=FULL).astype(HALF)
+        copy = remote(
+            pre_out.at[g], pre_in.at[g], pre_send.at[g], pre_recv.at[g], partner
+        )
+        copy.start()
+        early.append(copy)
+    for g in range(GROUPS):
+        near = zs[0, rows(g)].astype(HALF)
+        result = jnp.dot(near, col2[core], preferred_element_type=FULL)
+        early[g].wait()
+        dispatch(FORWARD, g, result + pre_in[g].astype(FULL))
+    later = [pass_on(0, log_mean, lm_far), pass_on(1, counts, cnt_far)]
+    fetch.wait()
+    regroup(row2)
+    later.append(pass_on(2, row2.at[1 - core], row_far))
+    later.append(pass_on(3, pos, zs.at[1]))
+    later.append(pass_on(4, mom, ps.at[1]))
+    later.append(pass_on(5, col2.at[1 - core], col_far))
+    for copy in later:
         copy.wait()
 
     def section(at, carry):
@@ -176,11 +236,22 @@
             )
         for g in range(GROUPS):
             pulled = expand(BACKWARD, g, col2, col_far)
-            size = step[rows(g)]
+            size = jnp.concatenate([step[rows(g)]] * (cells // step.shape[1]), axis=1)
             for part in range(2):
                 values = zs[part, rows(g)]
-                moment = ps[part, rows(g)] - weight * size * (values - pulled[part])
+                force = values - pulled[part]
+                moment = ps[part, rows(g)] - weight * size * force
                 ps[part, rows(g)] = moment
+
+                if part == 0:
+                    @pl.when(at == 1)
+                    def _():
+                        last_pos[rows(g)] = values
+                        mid_mom[rows(g)] = moment
+
+                    @pl.when(at == 2)
+                    def _():
+                        last_force[rows(g)] = force
 
                 @pl.when(at < 2)
                 def _():
@@ -203,8 +274,6 @@
     e_own[...] = jnp.broadcast_to(total, e_own.shape)
     copy = remote(e_own, e_far, tail_send.at[0], tail_recv.at[0], partner)
     copy.start()
-    new_pos[...] = zs[0]
-    new_mom[...] = after
     copy.wait()
     e_chip[...] = e_own[...] + e_far[...]
 
@@ -227,7 +296,8 @@
     copy = remote(e_part, e_rest, tail_send.at[1], tail_recv.at[1], partner)
     copy.start()
     copy.wait()
-    energy[...] = e_part[...] + e_rest[...]
+    energy[...] = e_part[...]
+    energy_rest[...] = e_rest[...]
 
 
 def on_device(
@@ -238,38 +308,35 @@
     tiles = tile_ranks.shape[0]
     halves = tiles // 2
     ranked = row_factors.shape[2]
-    device = lax.axis_index(("col", "row"))
-    tile = device // 2
-    levels = jnp.arange(ranked, dtype=jnp.int32)
-    col_ranks = lax.dynamic_slice_in_dim(tile_ranks, tile, 1, 1)[:, 0]
-    row_ranks = lax.dynamic_slice_in_dim(tile_ranks, tile, 1, 0)[0]
-
-    def prepare(factors, ranks):
-        live = levels[None, :] < ranks[:, None]
-        kept = jnp.where(live[None], factors, jnp.zeros_like(factors))
-        kept = kept.reshape(cells, halves, 2, ranked)
-        return jnp.transpose(kept, (2, 0, 1, 3)).reshape(2, cells, halves * ranked)
-
     block = chains // GROUPS
     vmem = pl.BlockSpec(memory_space=pltpu.VMEM)
     dma = pltpu.SemaphoreType.DMA
     small = pltpu.VMEM((8, chains), FULL)
-    new_pos, new_mom, energy = pl.pallas_call(
+    any_space = pl.BlockSpec(memory_space=pl.ANY)
+    big = jax.ShapeDtypeStruct(position.shape, FULL)
+    line = jax.ShapeDtypeStruct((8, chains), FULL)
+    last_pos, mid_mom, last_force, energy, energy_rest = pl.pallas_call(
         functools.partial(kernel, row_size),
-        out_shape=(
-            jax.ShapeDtypeStruct(position.shape, FULL),
-            jax.ShapeDtypeStruct(position.shape, FULL),
-            jax.ShapeDtypeStruct((8, chains), FULL),
-        ),
-        in_specs=[vmem] * 7,
-        out_specs=(vmem, vmem, vmem),
+        out_shape=(big, big, big, line, line),
+        in_specs=[
+            vmem, vmem, any_space, any_space,
+            pl.BlockSpec(memory_space=pltpu.SMEM), vmem, vmem, vmem,
+        ],
+        out_specs=(vmem,) * 5,
         scratch_shapes=[
             pltpu.VMEM((2, chains, cells), FULL),
             pltpu.VMEM((2, chains, cells), FULL),
+            pltpu.VMEM((cells, tiles, ranked), HALF),
+            pltpu.VMEM((2, cells, halves * ranked), HALF),
+            pltpu.VMEM((2, cells, halves * ranked), HALF),
             pltpu.VMEM((cells, halves * ranked), HALF),
             pltpu.VMEM((cells, halves * ranked), HALF),
             pltpu.VMEM((1, cells), FULL),
             pltpu.VMEM((1, cells), jnp.int32),
+            pltpu.VMEM((2, 1, halves * ranked), FULL),
+            pltpu.VMEM((chains, chains), FULL),
+            pltpu.VMEM((GROUPS, block, halves * ranked), HALF),
+            pltpu.VMEM((GROUPS, block, halves * ranked), HALF),
             pltpu.VMEM((2, GROUPS, halves, block, ranked), HALF),
             pltpu.VMEM((2, GROUPS, halves, block, ranked), HALF),
             pltpu.VMEM((2, GROUPS, 2, block, cells), SWAP),
@@ -278,7 +345,7 @@
             small, small, small,
             pltpu.VMEM((halves, 8, chains), FULL),
             small, small,
-            dma((6,)), dma((6,)),
+            dma((1,)), dma((6,)), dma((6,)), dma((GROUPS,)), dma((GROUPS,)),
             dma((2, GROUPS, halves)), dma((2, GROUPS, halves)),
             dma((2, GROUPS, 2)), dma((2, GROUPS, 2)),
             dma((2,)), dma((2,)),
@@ -286,11 +353,13 @@
         ],
         compiler_params=pltpu.CompilerParams(collective_id=0, has_side_effects=True),
     )(
-        position, momentum,
-        prepare(col_factors, col_ranks), prepare(row_factors, row_ranks),
-        log_mean[None, :], counts[None, :], step_size[:, None],
+        position, momentum, col_factors, row_factors, tile_ranks,
+        log_mean[None, :], counts[None, :], step_size[None, :],
     )
-    return new_pos, new_mom, energy[0]
+    full_step = step_size[:, None]
+    new_position = last_pos + full_step * mid_mom
+    new_momentum = mid_mom - 0.5 * full_step * last_force
+    return new_position, new_momentum, (energy + energy_rest)[0]
 
 
 def solution(mesh):

time: 87.4 us -> 72.9 us (0.83)
  local copies, waits for them, and re-layouts: 11.3 us -> 0.52 us
  Pallas kernels: 71.5 us -> 68.2 us
    reshape x4 -> x0, local copies, waits for them, and re-layouts: 5.19 us -> none  [the longest x2 4.65 us: prepare(): return jnp.transpose(kept, (2, 0, 1, 3)).reshape(2, cells, halves * ranked)]
    unnamed x6 -> x2, local copies, waits for them, and re-layouts: 4.02 us -> 0.01 us
    select_n x2 -> x0, other arithmetic: 3.46 us -> none  [prepare(): kept = jnp.where(live[None], factors, jnp.zeros_like(factors))]
    pallas_call x1, Pallas kernels: 71.5 us -> 68.2 us  [on_device(): pl.pallas_call(functools.partial(kernel, row_size), out_shape=(big, big,...]
    sub x0 -> x1, other arithmetic: none -> 2.01 us  [on_device(): new_momentum = mid_mom - 0.5 * full_step * last_force]
where the time goes in v2:
time: 72.9 us; the launch traced here: 72.7 us
  Pallas kernels  68.2 us (94%)
  other arithmetic  3.35 us (5%)
    pallas_call x1, Pallas kernels, on_device(): pl.pallas_call(functools.partial(kernel, row_size), out_shape=(big, big,...  68.2 us
    sub x1, other arithmetic, on_device(): new_momentum = mid_mom - 0.5 * full_step * last_force  2.01 us

profile of v2, /device:TPU:0, one launch (start us, length us, event | category | flops | bytes accessed | tf_op | source)
XLA Modules:
  0.0 72.7 jit_solution(470481733735716131)
XLA Ops:
  0.6 0.7 broadcast_multiply_fusion
  1.3 0.0 copy-start
  1.3 68.2 %shard_map.103 = (f32[128,512]{1,0:T(8,128)}, f32[128,512]{1,0:T(8,128)}, f32[128,512]{1,0:T(8,128)}, f32[8,128]{1,0:T(8,128)}, f32[8,128]{1,0:T(8,128)}) custom-call(f32[128,512]{1,0:T(8,128)} %pos.1, f32[128,512]{1,0:T(8,128)} %mom.1, bf16[512,16,128]{2,1,0:T(8,128)(2,1)} %col_raw.1, bf16[512,16,128]{2,1,0:T(8,128)(2,1)} %row_raw.1, s32[16,16]{1,0:T(8,128)} %ranks.1, ...), custom_call_target="tpu_custom_call" | custom-call | tf_op jit(solution)/shard_map/pallas_call | solution.py:318
  69.5 0.0 copy-done
  69.5 2.0 %multiply_subtract_fusion = (f32[128,512]{1,0:T(8,128)}, f32[128,512]{1,0:T(8,128)}) fusion(f32[128,512]{1,0:T(8,128)} %get-tuple-element.9, f32[128,512]{1,0:T(8,128)} %get-tuple-element.10, f32[128]{0:T(128)S(1)} %broadcast_multiply_fusion, f32[128,512]{1,0:T(8,128)} %get-tuple-element.8, f32[128]{0:T(128)S(1)} %copy-done), kind=kLoop, calls=%fused_computation | loop fusion | flops 262144 | bytes 1311744 | tf_op jit(solution)/shard_map/sub | solution.py:361
  71.5 0.7 add.7
  72.2 0.5 slice_bitcast_fusion
Async XLA Ops:
  1.3 68.2 %copy-start = (f32[128]{0:T(128)S(1)}, f32[128]{0:T(128)}, u32[]{:S(2)}) copy-start(f32[128]{0:T(128)} %param.15) | copy-start | bytes 1540

commit v3 on v2

--- a/solution.py
+++ b/solution.py
@@ -134,7 +134,7 @@
 
     def project(way, g, near, far, near_ref, far_ref):
         result = jnp.dot(near, near_ref[core], preferred_element_type=FULL)
-        result += jnp.dot(far, far_ref[...], preferred_element_type=FULL)
+        result += jnp.dot(far(), far_ref[...], preferred_element_type=FULL)
         dispatch(way, g, result)
 
     def dispatch(way, g, result):
@@ -180,16 +180,19 @@
             swap_send.at[way, g, 1], swap_recv.at[way, g, 1], partner,
         ))
         copies[1].start()
-        for copy in copies:
-            copy.wait()
+        copies[0].wait()
         near = near + swap_in[way, g, 0].astype(FULL)
-        far = far + swap_in[way, g, 1].astype(FULL)
-        return near, far
+
+        def rest():
+            copies[1].wait()
+            return far + swap_in[way, g, 1].astype(FULL)
+
+        return near, rest
 
     def send_forward(g):
         project(
             FORWARD, g,
-            zs[0, rows(g)].astype(HALF), zs[1, rows(g)].astype(HALF),
+            zs[0, rows(g)].astype(HALF), lambda: zs[1, rows(g)].astype(HALF),
             col2, col_far,
         )
 
@@ -226,9 +229,11 @@
             intensity = jnp.exp(exponent)
             rate = counts[...].astype(FULL)
             residual = (rate - intensity).astype(HALF)
-            residual_far = (
-                cnt_far[...].astype(FULL) - jnp.exp(lm_far[...] + far)
-            ).astype(HALF)
+
+            def residual_far():
+                intensity_far = jnp.exp(lm_far[...] + far())
+                return (cnt_far[...].astype(FULL) - intensity_far).astype(HALF)
+
             project(BACKWARD, g, residual, residual_far, row2, row_far)
             values = zs[0, rows(g)]
             gain[rows(g)] += sign * (
@@ -239,7 +244,7 @@
             size = jnp.concatenate([step[rows(g)]] * (cells // step.shape[1]), axis=1)
             for part in range(2):
                 values = zs[part, rows(g)]
-                force = values - pulled[part]
+                force = values - (pulled[0] if part == 0 else pulled[1]())
                 moment = ps[part, rows(g)] - weight * size * force
                 ps[part, rows(g)] = moment
 
@@ -358,8 +363,8 @@
     )
     full_step = step_size[:, None]
     new_position = last_pos + full_step * mid_mom
-    new_momentum = mid_mom - 0.5 * full_step * last_force
-    return new_position, new_momentum, (energy + energy_rest)[0]
+    new_momentum = mid_mom - full_step * (0.5 * last_force)
+    return new_position, new_momentum, energy[0] + energy_rest[0]
 
 
 def solution(mesh):

time: 72.9 us -> 71.9 us (0.986)
  Pallas kernels: 68.2 us -> 67.2 us
    pallas_call x1, Pallas kernels: 68.2 us -> 67.2 us  [on_device(): pl.pallas_call(functools.partial(kernel, row_size), out_shape=(big, big,...]
where the time goes in v3:
time: 71.9 us; the launch traced here: 71.7 us
  Pallas kernels  67.2 us (93%)
  other arithmetic  3.86 us (5%)
    pallas_call x1, Pallas kernels, on_device(): pl.pallas_call(functools.partial(kernel, row_size), out_shape=(big, big,...  67.2 us
    sub x1, other arithmetic, on_device(): new_momentum = mid_mom - full_step * (0.5 * last_force)  2.01 us

profile of v3, /device:TPU:0, one launch (start us, length us, event | category | flops | bytes accessed | tf_op | source)
XLA Modules:
  0.0 71.7 jit_solution(1960508726895206632)
XLA Ops:
  0.6 0.7 broadcast_multiply_fusion
  1.3 0.0 copy-start
  1.3 67.2 %shard_map.103 = (f32[128,512]{1,0:T(8,128)}, f32[128,512]{1,0:T(8,128)}, f32[128,512]{1,0:T(8,128)}, f32[8,128]{1,0:T(8,128)}, f32[8,128]{1,0:T(8,128)}) custom-call(f32[128,512]{1,0:T(8,128)} %pos.1, f32[128,512]{1,0:T(8,128)} %mom.1, bf16[512,16,128]{2,1,0:T(8,128)(2,1)} %col_raw.1, bf16[512,16,128]{2,1,0:T(8,128)(2,1)} %row_raw.1, s32[16,16]{1,0:T(8,128)} %ranks.1, ...), custom_call_target="tpu_custom_call" | custom-call | tf_op jit(solution)/shard_map/pallas_call | solution.py:323
  68.5 0.0 copy-done
  68.5 2.0 %multiply_subtract_fusion = (f32[128,512]{1,0:T(8,128)}, f32[128,512]{1,0:T(8,128)}) fusion(f32[128,512]{1,0:T(8,128)} %get-tuple-element.9, f32[128,512]{1,0:T(8,128)} %get-tuple-element.10, f32[128]{0:T(128)S(1)} %broadcast_multiply_fusion, f32[128,512]{1,0:T(8,128)} %get-tuple-element.8, f32[128]{0:T(128)S(1)} %copy-done), kind=kLoop, calls=%fused_computation | loop fusion | flops 262144 | bytes 1311744 | tf_op jit(solution)/shard_map/sub | solution.py:366
  70.5 1.2 %add_bitcast_fusion = f32[128]{0:T(128)} fusion(f32[8,128]{1,0:T(8,128)} %get-tuple-element.12, f32[8,128]{1,0:T(8,128)} %get-tuple-element.11), kind=kLoop, calls=%fused_computation.2 | loop fusion | flops 128 | bytes 1536 | tf_op jit(solution)/shard_map/add | solution.py:367
Async XLA Ops:
  1.3 67.2 %copy-start = (f32[128]{0:T(128)S(1)}, f32[128]{0:T(128)}, u32[]{:S(2)}) copy-start(f32[128]{0:T(128)} %param.15) | copy-start | bytes 1540

commit v4 on v3

--- a/solution.py
+++ b/solution.py
@@ -160,7 +160,12 @@
                 send.at[way, g, m], recv.at[way, g, m], peer(m),
             )
             copy.wait_recv()
-            copy.wait_send()
+
+        def release(m):
+            remote(
+                out_buf.at[way, g, m], in_buf.at[way, g, m],
+                send.at[way, g, m], recv.at[way, g, m], peer(m),
+            ).wait_send()
 
         each_peer(finish)
         held = jnp.concatenate([in_buf[way, g, m] for m in range(halves)], axis=1)
@@ -180,6 +185,7 @@
             swap_send.at[way, g, 1], swap_recv.at[way, g, 1], partner,
         ))
         copies[1].start()
+        each_peer(release)
         copies[0].wait()
         near = near + swap_in[way, g, 0].astype(FULL)
 

time: 71.9 us -> 72.7 us (1.011)
  Pallas kernels: 67.2 us -> 68 us
    pallas_call x1, Pallas kernels: 67.2 us -> 68 us  [on_device(): pl.pallas_call(functools.partial(kernel, row_size), out_shape=(big, big,...]
where the time goes in v4:
time: 72.7 us; the launch traced here: 72.5 us
  Pallas kernels  68 us (94%)
  other arithmetic  3.86 us (5%)
    pallas_call x1, Pallas kernels, on_device(): pl.pallas_call(functools.partial(kernel, row_size), out_shape=(big, big,...  68 us
    sub x1, other arithmetic, on_device(): new_momentum = mid_mom - full_step * (0.5 * last_force)  2.01 us

profile of v4, /device:TPU:0, one launch (start us, length us, event | category | flops | bytes accessed | tf_op | source)
XLA Modules:
  0.0 72.5 jit_solution(4243766283918780482)
XLA Ops:
  0.6 0.7 broadcast_multiply_fusion
  1.3 0.0 copy-start
  1.3 68.0 %shard_map.103 = (f32[128,512]{1,0:T(8,128)}, f32[128,512]{1,0:T(8,128)}, f32[128,512]{1,0:T(8,128)}, f32[8,128]{1,0:T(8,128)}, f32[8,128]{1,0:T(8,128)}) custom-call(f32[128,512]{1,0:T(8,128)} %pos.1, f32[128,512]{1,0:T(8,128)} %mom.1, bf16[512,16,128]{2,1,0:T(8,128)(2,1)} %col_raw.1, bf16[512,16,128]{2,1,0:T(8,128)(2,1)} %row_raw.1, s32[16,16]{1,0:T(8,128)} %ranks.1, ...), custom_call_target="tpu_custom_call" | custom-call | tf_op jit(solution)/shard_map/pallas_call | solution.py:329
  69.3 0.0 copy-done
  69.3 2.0 %multiply_subtract_fusion = (f32[128,512]{1,0:T(8,128)}, f32[128,512]{1,0:T(8,128)}) fusion(f32[128,512]{1,0:T(8,128)} %get-tuple-element.9, f32[128,512]{1,0:T(8,128)} %get-tuple-element.10, f32[128]{0:T(128)S(1)} %broadcast_multiply_fusion, f32[128,512]{1,0:T(8,128)} %get-tuple-element.8, f32[128]{0:T(128)S(1)} %copy-done), kind=kLoop, calls=%fused_computation | loop fusion | flops 262144 | bytes 1311744 | tf_op jit(solution)/shard_map/sub | solution.py:372
  71.3 1.2 %add_bitcast_fusion = f32[128]{0:T(128)} fusion(f32[8,128]{1,0:T(8,128)} %get-tuple-element.12, f32[8,128]{1,0:T(8,128)} %get-tuple-element.11), kind=kLoop, calls=%fused_computation.2 | loop fusion | flops 128 | bytes 1536 | tf_op jit(solution)/shard_map/add | solution.py:373
Async XLA Ops:
  1.3 68.0 %copy-start = (f32[128]{0:T(128)S(1)}, f32[128]{0:T(128)}, u32[]{:S(2)}) copy-start(f32[128]{0:T(128)} %param.15) | copy-start | bytes 1540
